TPU v7x, 512 devices: a whole 4x4x16 slice. The times are simulated.
512 devices in a mesh: section: 8 (over z_lo), dp: 32 (over x, y, core), tensor: 2 (over z_hi).
Axes of the slice: x: 4, y: 4, z: 16 (z_hi: 2, z_lo: 8; z = z_hi * 8 + z_lo), core: 2. Of those that a mesh axis runs over, the one named last changes fastest.
Arguments:
- hidden_in: bfloat16 [8, 4096, 8192], P('section', ('dp', 'tensor')), may hold values from -600 to 600
- norm_gain: bfloat16 [8, 8192], P('section'), may hold values from 0.5 to 1.5
- value_weight: bfloat16 [8, 8192, 512], P('section', 'dp', 'tensor'), may hold values from -0.0625 to 0.0625
- query_vectors: bfloat16 [8, 4096, 4096], P('section', 'dp', 'tensor'), may hold values from -9 to 9
- key_vectors: bfloat16 [8, 4096, 512], P('section', 'dp', 'tensor'), may hold values from -9 to 9
- grad_attn: bfloat16 [8, 4096, 4096], P('section', 'dp', 'tensor'), may hold values from -250 to 250
- positions: int32 [8, 4096], P('section', 'dp'), may hold values from 0 to 65535, as said below
Outputs:
- value_weight_grad: float32 [8, 8192, 512], P('section', 'dp', 'tensor')
- norm_gain_grad: float32 [8, 8192], P('section')
- to_previous: bfloat16 [8, 4096, 8192], P('section', ('dp', 'tensor'))
Inputs may be any that keep to these rules, and one draw needn't show every extreme that they name: Within each micro-batch of 128 rows, positions rise by one from row to row except at one row between row 32 and row 95, where a new document starts at position 0.
All inputs are finite; a program needn't handle non-finite values.
Results may differ from a plain program's by a relative error of at most 0.014.
Values may be sent and summed in bfloat16 or wider, within the bound.
No kernel may reach another device: no remote copies, remote signals or barrier semaphores. Data moves between devices by JAX's collectives and lax.ppermute only.
A program may use at most 64 MiB of HBM per device.

v0:
```python
import math
import jax
import jax.numpy as jnp
from jax import lax
from jax.sharding import PartitionSpec as P

HD = 128
QPK = 8


def shifted(value, axis, steps):
    count = lax.axis_size(axis)
    first, last = (max(0, -steps), min(count, count - steps))
    return lax.ppermute(value, axis, [(source, source + steps) for source in range(first, last)])


def attend(query_rows, key_rows, grad_rows, position_rows):
    length = query_rows.shape[0]
    groups = key_rows.shape[1] // HD
    query_heads = query_rows.reshape(length, groups, QPK, HD)
    key_heads = key_rows.reshape(length, groups, HD)
    grad_heads = grad_rows.reshape(length, groups, QPK, HD)
    scores = jnp.einsum(
        "igpd,jgd->gpij", query_heads, key_heads, preferred_element_type=jnp.float32
    ) / math.sqrt(HD)
    places = jnp.arange(length, dtype=jnp.int32)
    visible = (places[:, None] >= places[None, :]) & (
        position_rows[:, None] - position_rows[None, :] == places[:, None] - places[None, :]
    )
    masked = jnp.where(visible, scores, jnp.float32(-1e30))
    largest = jnp.max(masked, axis=-1, keepdims=True)
    powers = jnp.where(visible, jnp.exp(masked - largest), jnp.float32(0.0))
    probabilities = powers / jnp.sum(powers, axis=-1, keepdims=True)
    weights = probabilities.astype(jnp.bfloat16)
    value_grad = jnp.einsum(
        "gpij,igpd->jgd", weights, grad_heads, preferred_element_type=jnp.float32
    )
    return value_grad.reshape(length, groups * HD).astype(jnp.bfloat16)


def shards(hidden_in, norm_gain, value_weight, query_vectors, key_vectors, grad_attn, positions):
    rows_float = hidden_in[0].astype(jnp.float32)
    root_mean = jnp.sqrt(jnp.mean(rows_float * rows_float, axis=1, keepdims=True) + 1e-05)
    normed = rows_float / root_mean
    gain_float = norm_gain[0].astype(jnp.float32)
    own_input = (normed * gain_float).astype(jnp.bfloat16)
    layer_input = lax.all_gather(own_input, "tensor", axis=0, tiled=True)
    value_grad = attend(query_vectors[0], key_vectors[0], grad_attn[0], positions[0])
    local_weight = value_weight[0]
    weight_grad = lax.psum_scatter(
        jnp.einsum("tc,tk->ck", layer_input, value_grad, preferred_element_type=jnp.float32).astype(
            jnp.bfloat16
        ),
        "dp",
        scatter_dimension=0,
        tiled=True,
    ).astype(jnp.float32)
    input_part = jnp.einsum(
        "tk,ck->tc",
        value_grad,
        lax.all_gather(local_weight, "dp", axis=0, tiled=True),
        preferred_element_type=jnp.float32,
    ).astype(jnp.bfloat16)
    own_rows = hidden_in.shape[1]
    grad_input = lax.psum(input_part, "tensor").astype(jnp.float32)
    own_grad = lax.dynamic_slice_in_dim(
        grad_input, lax.axis_index("tensor") * own_rows, own_rows, 0
    )
    grad_normed = own_grad * gain_float
    inner_mean = jnp.mean(grad_normed * normed, axis=1, keepdims=True)
    grad_hidden = ((grad_normed - normed * inner_mean) / root_mean).astype(jnp.bfloat16)
    gain_grad = lax.psum(jnp.sum(own_grad * normed, axis=0), ("dp", "tensor"))
    to_previous = shifted(grad_hidden, "section", -1)
    return (weight_grad[None], gain_grad[None], to_previous[None])


def solution(mesh):
    placed = (
        P("section", ("dp", "tensor"), None),
        P("section", None),
        P("section", "dp", "tensor"),
        P("section", "dp", "tensor"),
        P("section", "dp", "tensor"),
        P("section", "dp", "tensor"),
        P("section", "dp"),
    )
    return jax.shard_map(
        shards,
        mesh=mesh,
        in_specs=placed,
        out_specs=(
            P("section", "dp", "tensor"),
            P("section", None),
            P("section", ("dp", "tensor"), None),
        ),
        check_vma=False,
    )
```

profile of v0, /device:TPU:32, one launch (start us, length us, event | category | flops | bytes accessed | tf_op | source)
XLA Modules:
  0.0 1020.2 jit_solution(7451055335804669944)
XLA Ops:
  7.2 0.0 copy-start.3
  7.2 0.0 all-gather.6.cloned.1.call-start
  7.2 0.7 all-gather.6.cloned.1.call-update
  7.9 0.0 all-reduce.2.cloned.1.call-start
  8.0 0.9 reshape_squeeze.9
  8.8 1.1 copy.20
  10.0 1.3 copy.19
  11.3 0.0 copy-done.3
  11.3 0.1 fusion.17
  11.4 0.5 fusion.29
  11.9 0.3 fusion.14
  12.2 64.4 %all-gather.6.cloned.1.call-done = bf16[1,8192,256]{2,1,0:T(8,128)(2,1)} async-done(((bf16[1,256,256]{2,1,0:T(8,128)(2,1)}), bf16[1,8192,256]{2,1,0:T(8,128)(2,1)}) %all-gather.6.cloned.1.call-update) | async-done | bytes 4194320 | tf_op jit(solution)/shard_map/all_gather | solution.py:61
  76.6 5.0 convolution_convert_fusion.1
  81.6 0.0 copy-start.2
  81.6 0.0 copy-start
  81.6 0.0 all-reduce.2.cloned.1.call-update
  81.6 0.0 all-gather.4.cloned.1.call-start
  81.7 0.7 copy-done.2
  82.4 0.4 copy-done
  82.9 0.3 fusion.8
  83.2 215.1 %all-reduce.2.cloned.1.call-done = bf16[128,8192]{1,0:T(8,128)(2,1)} async-done(((bf16[128,8192]{1,0:T(8,128)(2,1)}), bf16[128,8192]{1,0:T(8,128)(2,1)}) %all-reduce.2.cloned.1.call-update) | async-done | bytes 2097168 | tf_op jit(solution)/shard_map/psum | solution.py:65
  298.3 0.0 copy-start.1
  298.3 2.1 fusion.4
  300.4 0.0 copy-done.1
  300.4 1.6 fusion.6
  302.1 0.0 all-gather.4.cloned.1.call-update
  302.1 0.0 reduce-scatter.2.cloned.1.call-start
  302.1 112.5 %all-gather.4.cloned.1.call-done = bf16[128,8192]{1,0:T(8,128)(2,1)} async-done(((bf16[64,8192]{1,0:T(8,128)(2,1)}), bf16[128,8192]{1,0:T(8,128)(2,1)}) %all-gather.4.cloned.1.call-update) | async-done | bytes 2097168 | tf_op jit(solution)/shard_map/all_gather | solution.py:47
  414.6 4.8 convolution_convert_fusion
  419.4 0.0 reduce-scatter.2.cloned.1.call-update
  419.4 15.7 %collective-permute-start = (bf16[64,8192]{1,0:T(8,128)(2,1)S(1)}, bf16[64,8192]{1,0:T(8,128)(2,1)S(1)}, u32[]{:S(2)}, u32[]{:S(2)}) collective-permute-start(bf16[64,8192]{1,0:T(8,128)(2,1)S(1)} %get-tuple-element.5), channel_id=1, source_target_pairs={{64,0},{128,64},{192,128},{256,192},{320,256},{384,320},{448,384},... | collective-permute-start | bytes 3145736 | tf_op jit(solution)/shard_map/ppermute | solution.py:14
  435.2 575.9 %psum.15 = f32[1,8192]{1,0:T(1,128)} all-reduce(f32[1,8192]{1,0:T(1,128)S(1)} %bitcast.58), channel_id=1, replica_groups=mesh['section'=8,'dp'=32,'tensor'=2] {'dp','tensor'}, use_global_device_ids=true, to_apply=%region_6.7 | all-reduce | flops 8192 | bytes 65536 | tf_op jit(solution)/shard_map/psum | solution.py:72
  1011.1 0.0 collective-permute-done
  1011.1 0.0 reduce-scatter.2.cloned.1.call-done
  1011.1 1.6 bitcast_convert_fusion
  1012.7 1.0 copy.39
  (3 shorter events, 0.0 us)
Async XLA Ops:
  7.2 4.1 copy-start.3
  7.2 69.4 %all-gather.6.cloned.1.call-start = ((), (), s32[]{:S(2)}) async-start(), calls=%async_computation.4 | async-start | bytes 4325376 | tf_op jit(solution)/shard_map/all_gather | solution.py:61
  7.9 290.4 %all-reduce.2.cloned.1.call-start = ((), (), s32[]{:S(2)}) async-start(), calls=%async_computation.3 | async-start | bytes 4194304 | tf_op jit(solution)/shard_map/psum | solution.py:65
  81.6 0.8 copy-start.2
  81.6 1.2 copy-start
  81.6 333.0 %all-gather.4.cloned.1.call-start = ((), (), s32[]{:S(2)}) async-start(), calls=%async_computation.1 | async-start | bytes 3145728 | tf_op jit(solution)/shard_map/all_gather | solution.py:47
  298.3 2.1 copy-start.1
  302.1 709.0 %reduce-scatter.2.cloned.1.call-start = ((), (), s32[]{:S(2)}) async-start(), calls=%async_computation.2 | async-start | bytes 4325376 | tf_op jit(solution)/shard_map/reduce_scatter | solution.py:50
  419.4 591.6 %collective-permute-start = (bf16[64,8192]{1,0:T(8,128)(2,1)S(1)}, bf16[64,8192]{1,0:T(8,128)(2,1)S(1)}, u32[]{:S(2)}, u32[]{:S(2)}) collective-permute-start(bf16[64,8192]{1,0:T(8,128)(2,1)S(1)} %get-tuple-element.5), channel_id=1, source_target_pairs={{64,0},{128,64},{192,128},{256,192},{320,256},{384,320},{448,384},... | collective-permute-start | bytes 3145736 | tf_op jit(solution)/shard_map/ppermute | solution.py:14
Sparse Core Ops, SparseCore 0:
  11.1 65.4 all-gather.5
  81.8 216.4 all-reduce.1
  302.2 112.3 all-gather.3
  419.5 110.5 reduce-scatter.1
where the time goes:
time: 1020 us
  blocking collectives  576 us (56%)
  waiting for transfers between devices  393 us (39%)
  starting transfers between devices  15.9 us (2%)
  between operations  13.8 us (1%)
  matrix products  10.7 us (1%)
    psum x1, blocking collectives, shards(): gain_grad = lax.psum(jnp.sum(own_grad * normed, axis=0), ('dp', 'tensor'))  576 us
    psum x1, waiting for transfers between devices, shards(): grad_input = lax.psum(input_part, 'tensor').astype(jnp.float32)  215 us
    all_gather x1, waiting for transfers between devices, shards(): layer_input = lax.all_gather(own_input, 'tensor', axis=0, tiled=True)  112 us
    all_gather x1, waiting for transfers between devices, shards(): lax.all_gather(local_weight, 'dp', axis=0, tiled=True)  64.4 us
  transfers between devices with their start and end apart: 5, of which 3 were waited for; matrix products, arithmetic and copies ran while one was open for 0% of the time, Pallas kernels for 0%

commit v1 on v0

--- a/solution.py
+++ b/solution.py
@@ -69,7 +69,13 @@
     grad_normed = own_grad * gain_float
     inner_mean = jnp.mean(grad_normed * normed, axis=1, keepdims=True)
     grad_hidden = ((grad_normed - normed * inner_mean) / root_mean).astype(jnp.bfloat16)
-    gain_grad = lax.psum(jnp.sum(own_grad * normed, axis=0), ("dp", "tensor"))
+
+    def measure_panel(v0):
+        for m in ("dp", "tensor"):
+            v0 = jax.lax.psum(v0, axis_name=m)
+        return v0
+
+    gain_grad = measure_panel(jnp.sum(own_grad * normed, axis=0))
     to_previous = shifted(grad_hidden, "section", -1)
     return (weight_grad[None], gain_grad[None], to_previous[None])
 

time: 1020 us -> 589 us (0.58)
  blocking collectives: 576 us -> 144 us
    psum x1 -> x2, blocking collectives: 576 us -> 144 us  [measure_panel(): v0 = jax.lax.psum(v0, axis_name=m)]
  transfers between devices with their start and end apart: 5 -> 5, of which waited for: 3 -> 3; matrix products, arithmetic and copies ran while one was open for 0% -> 1% of each run, Pallas kernels for 0% -> 0%
where the time goes in v1:
time: 589 us
  waiting for transfers between devices  393 us (67%)
  blocking collectives  144 us (24%)
  starting transfers between devices  15.9 us (3%)
  between operations  13.9 us (2%)
  matrix products  10.7 us (2%)
    psum x1, waiting for transfers between devices, shards(): grad_input = lax.psum(input_part, 'tensor').astype(jnp.float32)  215 us
    psum x2, blocking collectives, measure_panel(): v0 = jax.lax.psum(v0, axis_name=m)  144 us
    all_gather x1, waiting for transfers between devices, shards(): layer_input = lax.all_gather(own_input, 'tensor', axis=0, tiled=True)  112 us
    all_gather x1, waiting for transfers between devices, shards(): lax.all_gather(local_weight, 'dp', axis=0, tiled=True)  64.4 us
    ppermute x1, starting transfers between devices, shifted(): lax.ppermute(value, axis, [(source, source + steps) for source in range(f...  15.7 us
  transfers between devices with their start and end apart: 5, of which 3 were waited for; matrix products, arithmetic and copies ran while one was open for 1% of the time, Pallas kernels for 0%

profile of v1, /device:TPU:32, one launch (start us, length us, event | category | flops | bytes accessed | tf_op | source)
XLA Modules:
  0.0 588.7 jit_solution(18445711897241856517)
XLA Ops:
  7.2 0.0 copy-start.3
  7.2 0.0 all-gather.6.cloned.1.call-start
  7.2 0.7 all-gather.6.cloned.1.call-update
  7.9 0.0 all-reduce.2.cloned.1.call-start
  8.0 0.9 reshape_squeeze.9
  8.8 1.1 copy.20
  10.0 1.3 copy.19
  11.3 0.0 copy-done.3
  11.3 0.1 fusion.17
  11.4 0.5 fusion.29
  11.9 0.3 fusion.14
  12.2 64.4 %all-gather.6.cloned.1.call-done = bf16[1,8192,256]{2,1,0:T(8,128)(2,1)} async-done(((bf16[1,256,256]{2,1,0:T(8,128)(2,1)}), bf16[1,8192,256]{2,1,0:T(8,128)(2,1)}) %all-gather.6.cloned.1.call-update) | async-done | bytes 4194320 | tf_op jit(solution)/shard_map/all_gather | solution.py:61
  76.6 5.0 convolution_convert_fusion.1
  81.6 0.0 copy-start.2
  81.6 0.0 copy-start
  81.6 0.0 all-reduce.2.cloned.1.call-update
  81.6 0.0 all-gather.4.cloned.1.call-start
  81.7 0.7 copy-done.2
  82.4 0.4 copy-done
  82.9 0.3 fusion.8
  83.2 215.1 %all-reduce.2.cloned.1.call-done = bf16[128,8192]{1,0:T(8,128)(2,1)} async-done(((bf16[128,8192]{1,0:T(8,128)(2,1)}), bf16[128,8192]{1,0:T(8,128)(2,1)}) %all-reduce.2.cloned.1.call-update) | async-done | bytes 2097168 | tf_op jit(solution)/shard_map/psum | solution.py:65
  298.3 0.0 copy-start.1
  298.3 2.1 fusion.4
  300.4 0.0 copy-done.1
  300.4 1.6 fusion.6
  302.1 0.0 all-gather.4.cloned.1.call-update
  302.1 0.0 reduce-scatter.2.cloned.1.call-start
  302.1 112.5 %all-gather.4.cloned.1.call-done = bf16[128,8192]{1,0:T(8,128)(2,1)} async-done(((bf16[64,8192]{1,0:T(8,128)(2,1)}), bf16[128,8192]{1,0:T(8,128)(2,1)}) %all-gather.4.cloned.1.call-update) | async-done | bytes 2097168 | tf_op jit(solution)/shard_map/all_gather | solution.py:47
  414.6 4.8 convolution_convert_fusion
  419.4 0.0 reduce-scatter.2.cloned.1.call-update
  419.4 15.7 %collective-permute-start = (bf16[64,8192]{1,0:T(8,128)(2,1)S(1)}, bf16[64,8192]{1,0:T(8,128)(2,1)S(1)}, u32[]{:S(2)}, u32[]{:S(2)}) collective-permute-start(bf16[64,8192]{1,0:T(8,128)(2,1)S(1)} %get-tuple-element.5), channel_id=1, source_target_pairs={{64,0},{128,64},{192,128},{256,192},{320,256},{384,320},{448,384},... | collective-permute-start | bytes 3145736 | tf_op jit(solution)/shard_map/ppermute | solution.py:14
  435.2 127.8 %psum.22 = f32[8192]{0:T(1024)S(1)} all-reduce(f32[8192]{0:T(1024)S(1)} %get-tuple-element.4), channel_id=1, replica_groups=mesh['section'=8,'dp'=32,'tensor'=2] {'dp'}, use_global_device_ids=true, to_apply=%region_6.7 | all-reduce | flops 8192 | bytes 65536 | tf_op jit(solution)/shard_map/psum | solution.py:75
  563.0 16.6 %psum.23 = f32[1,8192]{1,0:T(1,128)} all-reduce(f32[1,8192]{1,0:T(1,128)S(1)} %bitcast.58), channel_id=1, replica_groups=mesh['section'=8,'dp'=32,'tensor'=2] {'tensor'}, use_global_device_ids=true, to_apply=%region_7.8 | all-reduce | flops 8192 | bytes 65536 | tf_op jit(solution)/shard_map/psum | solution.py:75
  579.6 0.0 collective-permute-done
  579.6 0.0 reduce-scatter.2.cloned.1.call-done
  579.6 1.6 bitcast_convert_fusion
  581.2 1.0 copy.39
  (3 shorter events, 0.0 us)
Async XLA Ops:
  7.2 4.1 copy-start.3
  7.2 69.4 %all-gather.6.cloned.1.call-start = ((), (), s32[]{:S(2)}) async-start(), calls=%async_computation.4 | async-start | bytes 4325376 | tf_op jit(solution)/shard_map/all_gather | solution.py:61
  7.9 290.4 %all-reduce.2.cloned.1.call-start = ((), (), s32[]{:S(2)}) async-start(), calls=%async_computation.3 | async-start | bytes 4194304 | tf_op jit(solution)/shard_map/psum | solution.py:65
  81.6 0.8 copy-start.2
  81.6 1.2 copy-start
  81.6 333.0 %all-gather.4.cloned.1.call-start = ((), (), s32[]{:S(2)}) async-start(), calls=%async_computation.1 | async-start | bytes 3145728 | tf_op jit(solution)/shard_map/all_gather | solution.py:47
  298.3 2.1 copy-start.1
  302.1 277.5 %reduce-scatter.2.cloned.1.call-start = ((), (), s32[]{:S(2)}) async-start(), calls=%async_computation.2 | async-start | bytes 4325376 | tf_op jit(solution)/shard_map/reduce_scatter | solution.py:50
  419.4 160.1 %collective-permute-start = (bf16[64,8192]{1,0:T(8,128)(2,1)S(1)}, bf16[64,8192]{1,0:T(8,128)(2,1)S(1)}, u32[]{:S(2)}, u32[]{:S(2)}) collective-permute-start(bf16[64,8192]{1,0:T(8,128)(2,1)S(1)} %get-tuple-element.5), channel_id=1, source_target_pairs={{64,0},{128,64},{192,128},{256,192},{320,256},{384,320},{448,384},... | collective-permute-start | bytes 3145736 | tf_op jit(solution)/shard_map/ppermute | solution.py:14
Sparse Core Ops, SparseCore 0:
  11.1 65.4 all-gather.5
  81.8 216.4 all-reduce.1
  302.2 112.3 all-gather.3
  419.5 110.5 reduce-scatter.1
